TPU v7x, 32 devices: a whole 2x2x4 slice. The times are simulated.
32 devices in a mesh: macro: 8 (over z, y), pencil: 4 (over x, core).
Axes of the slice: x: 2, y: 2, z: 4, core: 2. Of those that a mesh axis runs over, the one named last changes fastest.
Arguments:
- voxel_material_ids: int32 [8, 128, 128, 128], P('macro', 'pencil'), may hold values from 0 to 2
- fiber_fraction: float32 [8, 128, 128, 128], P('macro', 'pencil'), may hold values from 0.5 to 18, as said below
- material_matrix_diffusivity: float32 [8, 3], P('macro'), may hold values from 0.2 to 5
- mesh_point_thermal_state: float32 [32], P('macro'), may hold values from 0.5 to 1.5
- element_corner_ids: int32 [8, 8], P('macro'), may hold values from 0 to 31, all different within a row
- global_entry_position: int32 [32], P('macro'), may hold values from 0 to 31, each once
- sample_choice_per_point: int32 [8], P('macro'), may hold values from 0 to 7, as said below
Outputs:
- qp_flux: float32 [8, 3], P('macro')
- nodal_flux: float32 [32], P('macro')
Inputs may be any that keep to these rules, and one draw needn't show every extreme that they name: `fiber_fraction`: positive. `sample_choice_per_point`: exactly 2 microstructures are used by 2 points each, 4 by 1 points each, and the rest by none.
All inputs are finite; a program needn't handle non-finite values.
Results may differ from a plain program's by a relative error of at most 0.0003.
Values sent between devices are 32-bit elements; how exact they have to be, the bound alone decides.
A program may use at most 64 MiB of HBM per device.

v0:
```python
import math

import jax
import jax.numpy as jnp
from jax import lax
from jax.sharding import PartitionSpec as P

PHASES = 3
ITERS = 2


HIGHEST = lax.Precision.HIGHEST


def passed_along(array, axis, by):
    size = lax.axis_size(axis)
    return lax.ppermute(array, axis, [(i, (i + by) % size) for i in range(size)])


def corner_signs():
    table = [
        [2.0 * (corner >> device_axis & 1) - 1.0 for device_axis in range(3)] for corner in range(8)
    ]
    return jnp.array(table, dtype=jnp.float32)


def base_field(voxel_material_ids, fiber_fraction, phase_lookup_table):
    conduct = jnp.zeros(fiber_fraction.shape, jnp.float32)
    for phase in range(PHASES):
        conduct = conduct + jnp.where(voxel_material_ids == phase, phase_lookup_table[phase], 0.0)
    return conduct * fiber_fraction


def fourier_tables(length):
    index = jnp.arange(length, dtype=jnp.int32)
    product = index[:, None] * index[None, :] % length
    angle = 2.0 * math.pi / length * product.astype(jnp.float32)
    return (jnp.cos(angle), jnp.sin(angle))


def complex_transform_pass(real_part, imag_part, cosine, sine, form, sign):
    real_cos = jnp.einsum(form, real_part, cosine, precision=HIGHEST)
    real_sin = jnp.einsum(form, real_part, sine, precision=HIGHEST)
    imag_cos = jnp.einsum(form, imag_part, cosine, precision=HIGHEST)
    imag_sin = jnp.einsum(form, imag_part, sine, precision=HIGHEST)
    return (real_cos - sign * imag_sin, imag_cos + sign * real_sin)


def forward_spectrum(field, cosine, sine):
    real_part = jnp.dot(field, cosine, precision=HIGHEST)
    imag_part = -jnp.dot(field, sine, precision=HIGHEST)
    real_part, imag_part = complex_transform_pass(
        real_part, imag_part, cosine, sine, "ink,nm->imk", -1.0
    )
    return complex_transform_pass(
        lax.all_to_all(real_part, "pencil", split_axis=1, concat_axis=0, tiled=True),
        lax.all_to_all(imag_part, "pencil", split_axis=1, concat_axis=0, tiled=True),
        cosine,
        sine,
        "nbk,nm->mbk",
        -1.0,
    )


def inverse_field(real_part, imag_part, cosine, sine):
    real_part, imag_part = complex_transform_pass(
        real_part, imag_part, cosine, sine, "nbk,nm->mbk", 1.0
    )
    real_part, imag_part = complex_transform_pass(
        lax.all_to_all(real_part, "pencil", split_axis=0, concat_axis=1, tiled=True),
        lax.all_to_all(imag_part, "pencil", split_axis=0, concat_axis=1, tiled=True),
        cosine,
        sine,
        "ink,nm->imk",
        1.0,
    )
    return jnp.dot(real_part, cosine, precision=HIGHEST) - jnp.dot(
        imag_part, sine, precision=HIGHEST
    )


def divergence(field, reference_k, gradient_field):
    contrast = field - reference_k
    polar = [contrast * gradient_field[device_axis] for device_axis in range(3)]
    below = passed_along(polar[0][-1:], "pencil", 1)
    behind = jnp.concatenate([below, polar[0][:-1]], axis=0)
    first = polar[0] - behind
    second = polar[1] - jnp.roll(polar[1], 1, axis=1)
    third = polar[2] - jnp.roll(polar[2], 1, axis=2)
    return first + second + third


def on_device(
    voxel_material_ids,
    fiber_fraction,
    material_matrix_diffusivity,
    mesh_point_thermal_state,
    element_corner_ids,
    global_entry_position,
    sample_choice_per_point,
):
    macro_index = lax.axis_index("macro")
    pencil_index = lax.axis_index("pencil")
    groups = lax.axis_size("macro")
    slab = fiber_fraction.shape[1]
    width = fiber_fraction.shape[3]
    volume = float(width**3)
    per_device = element_corner_ids.shape[0]
    cosine, sine = fourier_tables(width)
    conduct = base_field(voxel_material_ids[0], fiber_fraction[0], material_matrix_diffusivity[0])
    totals = lax.psum((jnp.sum(conduct), jnp.sum(conduct * conduct)), "pencil")
    stats = jnp.stack(totals).reshape(1, 2)
    mesh_point_flux_result = lax.all_gather(mesh_point_thermal_state, "macro", axis=0, tiled=True)
    rows_all, assign_all = (
        lax.all_gather(global_entry_position, "macro", axis=0, tiled=True),
        lax.all_gather(sample_choice_per_point, "macro", axis=0, tiled=True),
    )
    nodes = mesh_point_flux_result.shape[0]
    node_ids = jnp.arange(nodes, dtype=jnp.int32)
    picks = element_corner_ids[:, :, None] == node_ids
    fourier_argument = jnp.sum(jnp.where(picks, mesh_point_flux_result, 0.0), axis=2)
    rows = jnp.sum(jnp.where(picks, rows_all, 0), axis=2)
    signs = corner_signs()
    gradient = jnp.dot(fourier_argument, signs, precision=HIGHEST) / 4.0
    heat = jnp.sum(fourier_argument, axis=1) / 8.0
    gradients_all, heat_all, stats_all = (
        lax.all_gather(gradient, "macro", axis=0, tiled=True),
        lax.all_gather(heat, "macro", axis=0, tiled=True),
        lax.all_gather(stats, "macro", axis=0, tiled=True),
    )
    points = assign_all.shape[0]
    point_ids = jnp.arange(points, dtype=jnp.int32)
    same_group = assign_all[:, None] == assign_all[None, :]
    earlier = point_ids[None, :] < point_ids[:, None]
    rank = jnp.sum((same_group & earlier).astype(jnp.int32), axis=1)
    group_ids = jnp.arange(groups, dtype=jnp.int32)
    counts = jnp.sum((assign_all[None, :] == group_ids[:, None]).astype(jnp.int32), axis=1)
    loaded = counts == 2 * per_device
    vacant = counts == 0
    loaded_rank = jnp.cumsum(loaded.astype(jnp.int32)) - loaded.astype(jnp.int32)
    vacant_rank = jnp.cumsum(vacant.astype(jnp.int32)) - vacant.astype(jnp.int32)
    pairing = loaded[None, :] & vacant[:, None] & (loaded_rank[None, :] == vacant_rank[:, None])
    partner = jnp.sum(jnp.where(pairing, group_ids[None, :], 0), axis=1)
    helper = jnp.sum(jnp.where(pairing, group_ids[:, None], 0), axis=0)
    anchor = jnp.where(vacant, partner, group_ids)
    source = anchor[macro_index]
    offset = jnp.where(vacant[macro_index], per_device, 0)
    flat = conduct.reshape(groups, -1)
    spread = lax.all_to_all(flat, "macro", split_axis=0, concat_axis=0, tiled=True)
    chosen = jnp.take(spread, anchor, axis=0)
    kfield = lax.all_to_all(chosen, "macro", split_axis=0, concat_axis=0, tiled=True).reshape(
        conduct.shape
    )
    moved = loaded[assign_all] & (rank >= per_device)
    row_group = jnp.where(moved, helper[assign_all], assign_all)
    row_slot = jnp.where(moved, rank - per_device, rank)
    source_stats = stats_all[source]
    slot_ids = jnp.arange(per_device, dtype=jnp.int32)
    select = (assign_all[None, :] == source) & (rank[None, :] == offset + slot_ids[:, None])
    slot_gradient = jnp.sum(jnp.where(select[:, :, None], gradients_all[None, :, :], 0.0), axis=1)
    slot_heat = jnp.sum(jnp.where(select, heat_all[None, :], 0.0), axis=1)
    line_angle = 2.0 * math.pi / width * jnp.arange(width, dtype=jnp.int32).astype(jnp.float32)
    block_modes = pencil_index * slab + jnp.arange(slab, dtype=jnp.int32)
    block_angle = 2.0 * math.pi / width * block_modes.astype(jnp.float32)
    line_cos = jnp.cos(line_angle)
    block_cos = jnp.cos(block_angle)
    eigen = (
        (2.0 - 2.0 * line_cos)[:, None, None]
        + (2.0 - 2.0 * block_cos)[None, :, None]
        + (2.0 - 2.0 * line_cos)[None, None, :]
    )
    positive = eigen > 0
    inverse_eigen = jnp.where(positive, 1.0 / (volume * jnp.where(positive, eigen, 1.0)), 0.0)

    def solve_slot(carry, packed):
        point_gradient, point_heat = packed
        radiative = point_heat**3
        field = kfield + radiative
        mean_square = (
            source_stats[1] + 2.0 * radiative * source_stats[0]
        ) / volume + radiative * radiative
        reference_k = jnp.sqrt(mean_square)
        weight = inverse_eigen / reference_k
        gradient_field = [
            point_gradient[device_axis] + jnp.zeros_like(field) for device_axis in range(3)
        ]
        for sweep in range(ITERS):
            spectrum = forward_spectrum(
                divergence(field, reference_k, gradient_field), cosine, sine
            )
            potential = inverse_field(spectrum[0] * weight, spectrum[1] * weight, cosine, sine)
            above = passed_along(potential[:1], "pencil", -1)
            ahead = jnp.concatenate([potential[1:], above], axis=0)
            gradient_field = [
                point_gradient[0] + ahead - potential,
                point_gradient[1] + jnp.roll(potential, -1, axis=1) - potential,
                point_gradient[2] + jnp.roll(potential, -1, axis=2) - potential,
            ]
        local = jnp.stack(
            [jnp.sum(field * gradient_field[device_axis]) for device_axis in range(3)]
        )
        flux = lax.psum(local, "pencil") / volume
        return (carry, flux)

    ignored, slot_flux = lax.scan(solve_slot, jnp.float32(0.0), (slot_gradient, slot_heat))
    flux_all = lax.all_gather(slot_flux, "macro", axis=0, tiled=True)
    flux_row = row_group * per_device + row_slot
    mine = lax.dynamic_slice_in_dim(flux_row, macro_index * per_device, per_device)
    catalog = jnp.arange(flux_all.shape[0], dtype=jnp.int32)
    qp_flux = jnp.sum(
        jnp.where((mine[:, None] == catalog[None, :])[:, :, None], flux_all[None, :, :], 0.0),
        axis=1,
    )
    residual = jnp.dot(qp_flux, signs.T, precision=HIGHEST) / 4.0
    hits = rows[:, :, None] == node_ids
    local_rows = jnp.sum(jnp.where(hits, residual[:, :, None], 0.0), axis=(0, 1))
    nodal_flux = lax.psum_scatter(local_rows, "macro", scatter_dimension=0, tiled=True)
    return (qp_flux, nodal_flux)


def solution(mesh):
    in_specs = (
        P("macro", "pencil", None, None),
        P("macro", "pencil", None, None),
        P("macro", None),
        P("macro"),
        P("macro", None),
        P("macro"),
        P("macro"),
    )
    out_specs = (P("macro", None), P("macro"))
    return jax.shard_map(
        on_device, mesh=mesh, in_specs=in_specs, out_specs=out_specs, check_vma=False
    )
```

profile of v0, /device:TPU:0, one launch (start us, length us, event | category | flops | bytes accessed | tf_op | source)
XLA Modules:
  0.0 568.8 jit_solution(3135992971007034764)
XLA Ops:
  2.0 7.0 %fusion.336 = (f32[]{:T(128)}, f32[]{:T(128)}, f32[1,32,128,128]{3,2,1,0:T(8,128)}) fusion(f32[1,32,128,128]{3,2,1,0:T(8,128)} %param.9, f32[]{:T(128)} %bitcast.8, s32[1,32,128,128]{3,2,1,0:T(8,128)} %param.8, f32[]{:T(128)} %bitcast.7, f32[]{:T(128)} %bitcast.6), kind=kLoop, calls=%fused_computation.367 | loop fusion | flops 6291454 | bytes 6291476 | tf_op jit(solution)/shard_map/reduce_sum | solution.py:111
  9.0 7.4 %all-to-all-start = ((f32[8,1,65536]{2,1,0:T(1,128)}), f32[8,1,65536]{2,1,0:T(1,128)}, u32[]{:S(2)}, u32[]{:S(2)}) async-start(f32[8,1,65536]{2,1,0:T(1,128)} %bitcast.9), calls=%async_computation | async-start | bytes 4194304 | tf_op jit(solution)/shard_map/all_to_all | solution.py:149
  19.3 45.6 %all-reduce.9 = (s32[8]{0:T(128)S(1)}, s32[32]{0:T(128)S(1)}) all-reduce(s32[8]{0:T(128)S(1)} %dynamic-update-slice, s32[32]{0:T(128)S(1)} %dynamic-update-slice.6), channel_id=1, replica_groups=mesh['macro'=8,'pencil'=4] {'macro'}, use_global_device_ids=true, to_apply=%add | all-reduce | flops 40 | bytes 320
  80.0 7.4 %all-reduce.11 = (f32[1]{0:T(128)}, f32[1]{0:T(128)}) all-reduce(f32[1]{0:T(128)} %bitcast.29, f32[1]{0:T(128)} %bitcast.28), channel_id=1, replica_groups=mesh['macro'=8,'pencil'=4] {'pencil'}, use_global_device_ids=true, to_apply=%region_13.14 | all-reduce | flops 2 | bytes 16 | tf_op jit(solution)/shard_map/psum | solution.py:111
  90.4 40.0 %all-reduce.1 = f32[32]{0:T(128)S(1)} all-reduce(f32[32]{0:T(128)S(1)} %dynamic-update-slice.1), channel_id=1, replica_groups=mesh['macro'=8,'pencil'=4] {'macro'}, use_global_device_ids=true, to_apply=%add.1 | all-reduce | flops 32 | bytes 256
  132.8 26.2 %all-reduce.10 = (f32[8]{0:T(128)S(1)}, f32[8,2]{1,0:T(8,128)S(1)}, f32[24]{0:T(128)S(1)}) all-reduce(f32[8]{0:T(128)S(1)} %dynamic-update-slice.2, f32[8,2]{1,0:T(8,128)S(1)} %reshape.561, f32[24]{0:T(128)S(1)} %dynamic-update-slice.3), channel_id=1, replica_groups=mesh['macro'=8,'pencil'=4] {'macro'}, use_global_device_ids=true, to_apply=%add.2 | all-reduce | flops 48 | bytes 384
  191.7 4.4 all-to-all-start.2
  204.8 17.1 %all-to-all-done.2 = f32[32,128,128]{2,0,1:T(8,128)} async-done(((f32[32,128,128]{2,0,1:T(8,128)}), f32[32,128,128]{2,0,1:T(8,128)}, u32[]{:S(2)}, u32[]{:S(2)}) %all-to-all-start.2) | async-done | bytes 2097184 | tf_op jit(solution)/shard_map/while/body/eval_jaxpr/all_to_all | solution.py:56
  221.8 4.4 all-to-all-start.3
  229.7 22.4 %all-to-all-done.3 = f32[32,128,128]{2,0,1:T(8,128)} async-done(((f32[32,128,128]{2,0,1:T(8,128)}), f32[32,128,128]{2,0,1:T(8,128)}, u32[]{:S(2)}, u32[]{:S(2)}) %all-to-all-start.3) | async-done | bytes 2097184 | tf_op jit(solution)/shard_map/while/body/eval_jaxpr/all_to_all | solution.py:57
  270.4 4.4 all-to-all-start.5
  283.5 17.1 %all-to-all-done.5 = f32[128,32,128]{2,1,0:T(8,128)} async-done(((f32[128,32,128]{2,1,0:T(8,128)}), f32[128,32,128]{2,1,0:T(8,128)}, u32[]{:S(2)}, u32[]{:S(2)}) %all-to-all-start.5) | async-done | bytes 2097184 | tf_op jit(solution)/shard_map/while/body/eval_jaxpr/all_to_all | solution.py:71
  300.6 4.8 all-to-all-start.4
  314.3 16.5 %all-to-all-done.4 = f32[128,32,128]{2,1,0:T(8,128)} async-done(((f32[128,32,128]{2,1,0:T(8,128)}), f32[128,32,128]{2,1,0:T(8,128)}, u32[]{:S(2)}, u32[]{:S(2)}) %all-to-all-start.4) | async-done | bytes 2097184 | tf_op jit(solution)/shard_map/while/body/eval_jaxpr/all_to_all | solution.py:70
  377.5 17.1 %all-to-all-done.6 = f32[32,128,128]{2,0,1:T(8,128)} async-done(((f32[32,128,128]{2,0,1:T(8,128)}), f32[32,128,128]{2,0,1:T(8,128)}, u32[]{:S(2)}, u32[]{:S(2)}) %all-to-all-start.6) | async-done | bytes 2097184 | tf_op jit(solution)/shard_map/while/body/eval_jaxpr/all_to_all | solution.py:56
  394.6 4.4 all-to-all-start.7
  402.2 22.5 %all-to-all-done.7 = f32[32,128,128]{2,0,1:T(8,128)} async-done(((f32[32,128,128]{2,0,1:T(8,128)}), f32[32,128,128]{2,0,1:T(8,128)}, u32[]{:S(2)}, u32[]{:S(2)}) %all-to-all-start.7) | async-done | bytes 2097184 | tf_op jit(solution)/shard_map/while/body/eval_jaxpr/all_to_all | solution.py:57
  443.2 4.4 all-to-all-start.9
  456.2 17.1 %all-to-all-done.9 = f32[128,32,128]{2,1,0:T(8,128)} async-done(((f32[128,32,128]{2,1,0:T(8,128)}), f32[128,32,128]{2,1,0:T(8,128)}, u32[]{:S(2)}, u32[]{:S(2)}) %all-to-all-start.9) | async-done | bytes 2097184 | tf_op jit(solution)/shard_map/while/body/eval_jaxpr/all_to_all | solution.py:71
  473.3 4.7 all-to-all-start.8
  488.8 14.7 %all-to-all-done.8 = f32[128,32,128]{2,1,0:T(8,128)} async-done(((f32[128,32,128]{2,1,0:T(8,128)}), f32[128,32,128]{2,1,0:T(8,128)}, u32[]{:S(2)}, u32[]{:S(2)}) %all-to-all-start.8) | async-done | bytes 2097184 | tf_op jit(solution)/shard_map/while/body/eval_jaxpr/all_to_all | solution.py:70
  523.1 7.4 %psum.24 = f32[3]{0:T(128)S(1)} all-reduce(f32[3]{0:T(128)S(1)} %pad_maximum_fusion), channel_id=1, replica_groups=mesh['macro'=8,'pencil'=4] {'pencil'}, use_global_device_ids=true, to_apply=%region_17.18 | all-reduce | flops 3 | bytes 24 | tf_op jit(solution)/shard_map/while/body/eval_jaxpr/psum | solution.py:202
  531.3 17.1 %all-reduce.5 = f32[24]{0:T(128)S(1)} all-reduce(f32[24]{0:T(128)S(1)} %multiply_dynamic-update-slice_fusion), channel_id=4, replica_groups=mesh['macro'=8,'pencil'=4] {'macro'}, use_global_device_ids=true, to_apply=%add.5 | all-reduce | flops 24 | bytes 192
  548.8 19.1 %all-reduce.8 = f32[32]{0:T(128)S(1)} all-reduce(f32[32]{0:T(128)S(1)} %select_reduce_fusion.2), channel_id=5, replica_groups=mesh['macro'=8,'pencil'=4] {'macro'}, use_global_device_ids=true, to_apply=%region_21.22.clone | all-reduce | flops 32 | bytes 256
  (199 shorter events, 203.8 us)
Async XLA Ops:
  9.0 8.1 %copy-start.20 = (u32[32]{0:T(128)S(1)}, u32[32]{0:T(128)}, u32[]{:S(2)}) copy-start(u32[32]{0:T(128)} %constant.122) | copy-start | bytes 388
  9.0 9.4 %copy-start.23 = (s32[4]{0:T(128)S(1)}, s32[4]{0:T(128)}, u32[]{:S(2)}) copy-start(s32[4]{0:T(128)} %param.13) | copy-start | bytes 52
  9.0 56.7 %all-to-all-start = ((f32[8,1,65536]{2,1,0:T(1,128)}), f32[8,1,65536]{2,1,0:T(1,128)}, u32[]{:S(2)}, u32[]{:S(2)}) async-start(f32[8,1,65536]{2,1,0:T(1,128)} %bitcast.9), calls=%async_computation | async-start | bytes 4194304 | tf_op jit(solution)/shard_map/all_to_all | solution.py:149
  76.3 13.9 %copy-start.24 = (f32[4]{0:T(128)S(1)}, f32[4]{0:T(128)}, u32[]{:S(2)}) copy-start(f32[4]{0:T(128)} %param.11) | copy-start | bytes 52
  76.3 54.2 %copy-start.22 = (s32[1,8]{1,0:T(1,128)S(1)}, s32[1,8]{1,0:T(1,128)}, u32[]{:S(2)}) copy-start(s32[1,8]{1,0:T(1,128)} %param.12) | copy-start | bytes 100
  76.3 56.2 %copy-start.19 = (f32[8,3]{1,0:T(8,128)S(1)}, f32[8,3]{1,0:T(8,128)}, u32[]{:S(2)}) copy-start(f32[8,3]{1,0:T(8,128)} %constant.112.clone) | copy-start | bytes 292
  76.3 92.3 %all-to-all-start.1 = ((f32[8,1,65536]{2,1,0:T(1,128)}), f32[8,1,65536]{2,1,0:T(1,128)S(1)}, u32[]{:S(2)}, u32[]{:S(2)}) async-start(f32[8,1,65536]{2,1,0:T(1,128)} %copy.164), calls=%async_computation.1 | async-start | bytes 4194304 | tf_op jit(solution)/shard_map/all_to_all | solution.py:151
  174.3 3.9 collective-permute-start
  182.0 4.4 copy-start
  191.7 30.2 %all-to-all-start.2 = ((f32[32,128,128]{2,0,1:T(8,128)}), f32[32,128,128]{2,0,1:T(8,128)}, u32[]{:S(2)}, u32[]{:S(2)}) async-start(f32[32,128,128]{2,0,1:T(8,128)} %copy.167), calls=%async_computation.2 | async-start | bytes 4194304 | tf_op jit(solution)/shard_map/while/body/eval_jaxpr/all_to_all | solution.py:56
  221.8 30.2 %all-to-all-start.3 = ((f32[32,128,128]{2,0,1:T(8,128)}), f32[32,128,128]{2,0,1:T(8,128)}, u32[]{:S(2)}, u32[]{:S(2)}) async-start(f32[32,128,128]{2,0,1:T(8,128)} %copy.172), calls=%async_computation.3 | async-start | bytes 4194304 | tf_op jit(solution)/shard_map/while/body/eval_jaxpr/all_to_all | solution.py:57
  270.4 30.2 %all-to-all-start.5 = ((f32[128,32,128]{2,1,0:T(8,128)}), f32[128,32,128]{2,1,0:T(8,128)}, u32[]{:S(2)}, u32[]{:S(2)}) async-start(f32[128,32,128]{2,1,0:T(8,128)} %copy.184), calls=%async_computation.5 | async-start | bytes 4194304 | tf_op jit(solution)/shard_map/while/body/eval_jaxpr/all_to_all | solution.py:71
  274.8 3.9 copy-start.9
  300.6 30.2 %all-to-all-start.4 = ((f32[128,32,128]{2,1,0:T(8,128)}), f32[128,32,128]{2,1,0:T(8,128)}, u32[]{:S(2)}, u32[]{:S(2)}) async-start(f32[128,32,128]{2,1,0:T(8,128)} %copy.179), calls=%async_computation.4 | async-start | bytes 4194304 | tf_op jit(solution)/shard_map/while/body/eval_jaxpr/all_to_all | solution.py:70
  341.4 2.0 collective-permute-start.1
  347.2 3.8 collective-permute-start.2
  354.8 4.4 copy-start.2
  364.4 30.2 %all-to-all-start.6 = ((f32[32,128,128]{2,0,1:T(8,128)}), f32[32,128,128]{2,0,1:T(8,128)}, u32[]{:S(2)}, u32[]{:S(2)}) async-start(f32[32,128,128]{2,0,1:T(8,128)} %copy.191), calls=%async_computation.6 | async-start | bytes 4194304 | tf_op jit(solution)/shard_map/while/body/eval_jaxpr/all_to_all | solution.py:56
  394.6 30.2 %all-to-all-start.7 = ((f32[32,128,128]{2,0,1:T(8,128)}), f32[32,128,128]{2,0,1:T(8,128)}, u32[]{:S(2)}, u32[]{:S(2)}) async-start(f32[32,128,128]{2,0,1:T(8,128)} %copy.196), calls=%async_computation.7 | async-start | bytes 4194304 | tf_op jit(solution)/shard_map/while/body/eval_jaxpr/all_to_all | solution.py:57
  443.2 30.2 %all-to-all-start.9 = ((f32[128,32,128]{2,1,0:T(8,128)}), f32[128,32,128]{2,1,0:T(8,128)}, u32[]{:S(2)}, u32[]{:S(2)}) async-start(f32[128,32,128]{2,1,0:T(8,128)} %copy.208), calls=%async_computation.9 | async-start | bytes 4194304 | tf_op jit(solution)/shard_map/while/body/eval_jaxpr/all_to_all | solution.py:71
  447.6 3.9 copy-start.7
  473.3 30.2 %all-to-all-start.8 = ((f32[128,32,128]{2,1,0:T(8,128)}), f32[128,32,128]{2,1,0:T(8,128)}, u32[]{:S(2)}, u32[]{:S(2)}) async-start(f32[128,32,128]{2,1,0:T(8,128)} %copy.203), calls=%async_computation.8 | async-start | bytes 4194304 | tf_op jit(solution)/shard_map/while/body/eval_jaxpr/all_to_all | solution.py:70
  514.3 2.0 collective-permute-start.3
  548.6 19.9 %copy-start.21 = (f32[3]{0:T(128)}, f32[3]{0:T(128)S(1)}, u32[]{:S(2)}) copy-start(f32[3]{0:T(128)S(1)} %select_reduce_fusion.4) | copy-start | bytes 40
  (15 other events, 36.3 us)
where the time goes:
time: 577 us; the launch traced here: 569 us
  blocking collectives  163 us (28%)
  waiting for transfers between devices  150 us (26%)
  matrix products  102 us (18%)
  local copies, waits for them, and re-layouts  61.3 us (11%)
  starting transfers between devices  49.1 us (9%)
  other arithmetic  31.9 us (6%)
  between operations  11.5 us (2%)
    unnamed x5, blocking collectives  148 us
    all_to_all x2, waiting for transfers between devices, forward_spectrum(): lax.all_to_all(imag_part, 'pencil', split_axis=1, concat_axis=0, tiled=True)  44.9 us
    all_to_all x2, waiting for transfers between devices, inverse_field(): lax.all_to_all(imag_part, 'pencil', split_axis=0, concat_axis=1, tiled=True)  34.2 us
    all_to_all x2, waiting for transfers between devices, forward_spectrum(): lax.all_to_all(real_part, 'pencil', split_axis=1, concat_axis=0, tiled=True)  34.1 us
    all_to_all x2, waiting for transfers between devices, inverse_field(): lax.all_to_all(real_part, 'pencil', split_axis=0, concat_axis=1, tiled=True)  31.2 us
    dot_general x8, matrix products, complex_transform_pass(): real_sin = jnp.einsum(form, real_part, sine, precision=HIGHEST)  21.8 us
    dot_general x8, matrix products, complex_transform_pass(): imag_sin = jnp.einsum(form, imag_part, sine, precision=HIGHEST)  21.1 us
    dot_general x8, matrix products, complex_transform_pass(): real_cos = jnp.einsum(form, real_part, cosine, precision=HIGHEST)  20.8 us
  transfers between devices with their start and end apart: 14, of which 12 were waited for; matrix products, arithmetic and copies ran while one was open for 13% of the time, Pallas kernels for 0%

commit v1 on v0

v1 whole, which is shorter than its diff:
```python
import functools
import math

import jax
import jax.numpy as jnp
import numpy as np
from jax import lax
from jax.experimental import pallas as pl
from jax.experimental.pallas import tpu as pltpu
from jax.sharding import PartitionSpec as P

PHASES = 3
MESH = pl.DeviceIdType.MESH
F32 = jnp.float32
BF16 = jnp.bfloat16
GROUP = 4
STATS = 16
PAD = 8
BLOCK = 32


def hartley_tables(width):
    index = np.arange(width)
    angle = 2.0 * math.pi / width * (index[:, None] * index[None, :] % width)
    table = np.cos(angle) + np.sin(angle)
    high = table.astype(BF16)
    low = (table - high.astype(np.float64)).astype(BF16)
    right = np.concatenate([np.concatenate([high, low], axis=1)] * 2, axis=0)
    return right, np.ascontiguousarray(right.T)


def mode_tables(width, slab):
    line = 4.0 * np.sin(math.pi * np.arange(width) / width) ** 2
    lam = line[:, None] + line[None, :]
    safe = np.where(lam > 0, lam, 1.0)
    half = 1.0 + safe / 2.0
    root = half - np.sqrt(half * half - 1.0)
    scale = 1.0 / (1.0 / root - root) / width**2
    root[0, 0] = 1.0
    scale[0, 0] = 1.0 / width**3
    closing = 1.0 / (1.0 - np.where(lam > 0, root**width, 0.0))
    closing[0, 0] = 0.0
    return np.stack([root, scale, root**slab, closing]).astype(np.float32)


def split(x):
    high = x.astype(BF16)
    return high, (x - high.astype(F32)).astype(BF16)


def hartley_plane_pass(x, right, left):
    count, width = x.shape[0], x.shape[2]
    high, low = split(x.reshape(count * width, width))
    both = jnp.dot(jnp.concatenate([high, low], axis=1), right, preferred_element_type=F32)
    both = both[:, :width] + both[:, width:]
    planes = []
    for pair in range(count // 2):
        first = both[2 * pair * width : (2 * pair + 1) * width]
        second = both[(2 * pair + 1) * width : (2 * pair + 2) * width]
        high, low = split(jnp.concatenate([first, second], axis=1))
        result = jnp.dot(left, jnp.concatenate([high, low], axis=0), preferred_element_type=F32)
        result = result[:width] + result[width:]
        planes += [result[:, :width], result[:, width:]]
    return planes


def fold(x):
    return jnp.sum(x.reshape(-1, 8, x.shape[-1]), axis=0)


def kernel(
    ids_hbm,
    fiber_hbm,
    phase_ref,
    theta_ref,
    corner_ref,
    position_ref,
    choice_ref,
    right_ref,
    left_ref,
    modes_ref,
    out_ref,
    ids_ref,
    conduct_ref,
    spectrum_ref,
    line_ref,
    field_ref,
    moment_ref,
    info_ref,
    part_ref,
    stat_ref,
    load_sem,
    moment_send,
    moment_recv,
    info_send,
    info_recv,
    part_send,
    part_recv,
    stat_send,
    stat_recv,
):
    groups, slabs = lax.axis_size("macro"), lax.axis_size("pencil")
    macro, pencil = lax.axis_index("macro"), lax.axis_index("pencil")
    slab, width = conduct_ref.shape[0], conduct_ref.shape[2]
    owned = theta_ref.shape[0]
    volume = float(width) ** 3

    def loads(step):
        planes = pl.ds(step * GROUP, GROUP)
        return (
            pltpu.make_async_copy(ids_hbm.at[0, planes], ids_ref.at[planes], load_sem.at[0, step]),
            pltpu.make_async_copy(
                fiber_hbm.at[0, planes], conduct_ref.at[planes], load_sem.at[1, step]
            ),
        )

    for step in range(slab // GROUP):
        for load in loads(step):
            load.start()

    barrier = pltpu.get_barrier_semaphore()
    for k in range(1, slabs):
        pl.semaphore_signal(
            barrier, inc=1, device_id={"pencil": lax.rem(pencil + k, slabs)}, device_id_type=MESH
        )
    for k in range(1, groups):
        pl.semaphore_signal(
            barrier, inc=1, device_id={"macro": lax.rem(macro + k, groups)}, device_id_type=MESH
        )

    def ring(axis, here, size, source, target, send_sem, recv_sem):
        return [
            pltpu.make_async_remote_copy(
                src_ref=source,
                dst_ref=target(k),
                send_sem=send_sem.at[k],
                recv_sem=recv_sem.at[k],
                device_id={axis: lax.rem(here + k, size)},
                device_id_type=MESH,
            )
            for k in range(1, size)
        ]

    lane = lax.broadcasted_iota(jnp.int32, (1, 128), 1)
    hits = [jnp.where(lane == corner_ref[0, a], 1.0, 0.0) for a in range(8)]
    info = []
    for d in range(3):
        info.append(sum(hits[a] * (0.5 * (a >> d & 1) - 0.25) for a in range(8)))
    info.append(sum(hits) * 0.125)
    temperatures = jnp.zeros((1, 128), F32)
    rows = jnp.zeros((1, 128), F32)
    for n in range(owned):
        mine = lane == macro * owned + n
        temperatures = jnp.where(mine, theta_ref[n], temperatures)
        rows = jnp.where(mine, position_ref[n].astype(F32) + 1.0, rows)
    info += [temperatures, rows, jnp.zeros((1, 128), F32) + choice_ref[0].astype(F32)]
    info.append(jnp.zeros((1, 128), F32))
    info_ref[0] = jnp.concatenate(info, axis=0)

    def forward(step, carry):
        total, square = carry
        for load in loads(step):
            load.wait()
        planes = pl.ds(step * GROUP, GROUP)
        ids = ids_ref[planes]
        value = jnp.where(ids == 0, phase_ref[0, 0], phase_ref[0, PHASES - 1])
        for phase in range(1, PHASES - 1):
            value = jnp.where(ids == phase, phase_ref[0, phase], value)
        value = value * conduct_ref[planes]
        conduct_ref[planes] = value
        flat = value.reshape(GROUP * width, width)
        total = total + fold(flat)
        square = square + fold(flat * flat)
        scale = modes_ref[1]
        for i, plane in enumerate(hartley_plane_pass(value, right_ref[...], left_ref[...])):
            spectrum_ref[step * GROUP + i] = plane * scale
        return total, square

    zero = jnp.zeros((8, 128), F32)
    total, square = lax.fori_loop(0, slab // GROUP, forward, (zero, zero))

    def moments(block, carry):
        at = pl.ds(pl.multiple_of(block * BLOCK, BLOCK), BLOCK)
        root = modes_ref[0, at]
        power = jnp.ones_like(root)
        head = spectrum_ref[0, at]
        tail = head
        for x in range(1, slab):
            plane = spectrum_ref[x, at]
            power = power * root
            head = head + power * plane
            tail = plane + root * tail
        moment_ref[0, 0, at] = head
        moment_ref[0, 1, at] = tail
        return carry

    lax.fori_loop(0, width // BLOCK, moments, 0)

    pl.semaphore_wait(barrier, groups + slabs - 2)
    moment_copies = ring(
        "pencil", pencil, slabs, moment_ref.at[0], lambda k: moment_ref.at[k], moment_send, moment_recv
    )
    info_copies = ring(
        "macro", macro, groups, info_ref.at[0], lambda k: info_ref.at[k], info_send, info_recv
    )
    for copy in moment_copies + info_copies:
        copy.start()
    for copy in moment_copies:
        copy.wait()

    corner = sum(moment_ref[k, 0, :8, :] for k in range(slabs))
    first = (lax.broadcasted_iota(jnp.int32, (8, width), 0) == 0) & (
        lax.broadcasted_iota(jnp.int32, (8, width), 1) == 0
    )
    mean = jnp.sum(jnp.where(first, corner, 0.0))

    def solve(block, carry):
        at = pl.ds(pl.multiple_of(block * BLOCK, BLOCK), BLOCK)
        root, reach, closing = modes_ref[0, at], modes_ref[2, at], modes_ref[3, at]
        before = jnp.zeros_like(root)
        after = jnp.zeros_like(root)
        for i in range(slabs, 0, -1):
            before = before * reach + moment_ref[i % slabs, 1, at]
            after = after * reach + moment_ref[slabs - i, 0, at]
        before = before * closing
        after = after * closing
        back = after
        for x in range(slab - 1, -1, -1):
            back = root * back
            line_ref[x + 1, at] = back
            back = spectrum_ref[x, at] + back
        line_ref[0, at] = before + root * back
        ahead = before
        for x in range(slab):
            ahead = spectrum_ref[x, at] + root * ahead
            line_ref[x + 1, at] = line_ref[x + 1, at] + ahead
        line_ref[slab + 1, at] = root * ahead + after
        return carry

    lax.fori_loop(0, width // BLOCK, solve, 0)

    def place(x, plane):
        field_ref[x, PAD : PAD + width, :] = plane
        field_ref[x, PAD - 1 : PAD, :] = plane[width - 1 : width]
        field_ref[x, PAD + width : PAD + width + 1, :] = plane[:1]

    def backward(step, carry):
        planes = hartley_plane_pass(
            line_ref[pl.ds(1 + step * GROUP, GROUP)], right_ref[...], left_ref[...]
        )
        for i, plane in enumerate(planes):
            place(1 + step * GROUP + i, plane)
        return carry

    lax.fori_loop(0, slab // GROUP, backward, 0)
    edges = jnp.concatenate([line_ref[0:1], line_ref[slab + 1 : slab + 2]], axis=0)
    for x, plane in zip((0, slab + 1), hartley_plane_pass(edges, right_ref[...], left_ref[...])):
        place(x, plane)

    def lower(x):
        return pltpu.roll(x, 1, 1)

    def upper(x):
        return pltpu.roll(x, width - 1, 1)

    pairs = ((0, 0), (1, 1), (2, 2), (0, 1), (0, 2), (1, 2))

    def contract(x, sums):
        sums = list(sums)
        for block in range(width // BLOCK):

            def at(plane, shift):
                return field_ref[plane, PAD + block * BLOCK + shift : PAD + (block + 1) * BLOCK + shift, :]

            here, south, north = at(x + 1, 0), at(x + 1, -1), at(x + 1, 1)
            east, east_south = at(x + 2, 0), at(x + 2, -1)
            west, west_north = at(x, 0), at(x, 1)
            value = conduct_ref[x, block * BLOCK : (block + 1) * BLOCK, :]
            in_y, next_y = here - south, north - here
            out_x, into_x = east - here, here - west
            yy = next_y - in_y
            zz = (upper(here) - here) - (here - lower(here))
            second = [
                [mean - value - yy - zz, (east - east_south) - in_y, out_x - lower(out_x)],
                [next_y - (west_north - west), yy, next_y - lower(next_y)],
                [upper(into_x) - into_x, upper(in_y) - in_y, zz],
            ]
            weighted = [[value * second[e][d] for d in range(3)] for e in range(3)]
            for i, (d, f) in enumerate(pairs):
                product = sum(weighted[e][d] * second[e][f] for e in range(3))
                sums[i] = sums[i] + fold(product)
                sums[6 + i] = sums[6 + i] + fold(weighted[f][d])
        return tuple(sums)

    sums = lax.fori_loop(0, slab, contract, (zero,) * 12)
    tiles = [total, square, *sums, zero, zero]
    part_ref[pencil] = jnp.concatenate(
        [jnp.sum(tile, axis=0, keepdims=True) for tile in tiles], axis=0
    )
    part_copies = ring(
        "pencil", pencil, slabs, part_ref.at[pencil], lambda k: part_ref.at[pencil], part_send, part_recv
    )
    for copy in part_copies:
        copy.start()
    for copy in info_copies:
        copy.wait()
    theta = sum(info_ref[k, 4:5, :] for k in range(groups))
    target = sum(info_ref[k, 5:6, :] for k in range(groups))
    for copy in part_copies:
        copy.wait_send()
    for k in range(1, slabs):
        origin = lax.rem(pencil - k + slabs, slabs)
        pltpu.make_async_remote_copy(
            src_ref=part_ref.at[pencil],
            dst_ref=part_ref.at[origin],
            send_sem=part_send.at[k],
            recv_sem=part_recv.at[k],
            device_id={"pencil": origin},
            device_id_type=MESH,
        ).wait_recv()
    whole = sum(part_ref[s] for s in range(slabs))
    stat_ref[0] = jnp.zeros((STATS, 128), F32) + jnp.sum(whole, axis=1, keepdims=True)
    stat_copies = ring(
        "macro", macro, groups, stat_ref.at[0], lambda k: stat_ref.at[k], stat_send, stat_recv
    )
    for copy in stat_copies:
        copy.start()
    for copy in stat_copies:
        copy.wait()

    owners = [lax.rem(macro - k + groups, groups).astype(F32) for k in range(groups)]
    nodes = jnp.zeros((1, 128), F32)
    for q in range(groups):
        weights = info_ref[q]
        local = jnp.zeros((8, 128), F32) + jnp.sum(weights * theta, axis=1, keepdims=True)
        gradient = [local[d : d + 1] for d in range(3)]
        radiative = local[3:4] * local[3:4] * local[3:4]
        choice = weights[6:7]
        stats = jnp.zeros((STATS, 128), F32)
        for k in range(groups):
            stats = stats + jnp.where(choice == owners[k], stat_ref[k], 0.0)
        stats = stats * (1.0 / volume)
        average = stats[0:1]
        square_mean = stats[1:2] + 2.0 * radiative * average + radiative * radiative
        reference_k = jnp.sqrt(square_mean)
        factor = radiative - 2.0 * reference_k
        response = {}
        for i, (d, f) in enumerate(pairs):
            value = (stats[2 + i : 3 + i] - factor * stats[8 + i : 9 + i]) / square_mean
            response[d, f] = response[f, d] = value
        for d in range(3):
            flux = (average + radiative) * gradient[d]
            flux = flux + sum(response[d, e] * gradient[e] for e in range(3))
            nodes = nodes + flux * weights[d : d + 1]
            if q == 0:
                out_ref[d : d + 1, :] = flux
    for n in range(owned):
        wanted = (macro * owned + n + 1).astype(F32)
        row = jnp.sum(jnp.where(target == wanted, nodes, 0.0), axis=1, keepdims=True)
        out_ref[3 + n : 4 + n, :] = jnp.zeros((1, 128), F32) + row


def on_device(right, left, modes, groups, slabs, ids, fiber, phases, theta, corners, positions, choices):
    slab, width = fiber.shape[1], fiber.shape[3]
    owned = theta.shape[0]
    assert corners.shape[0] == 1 and groups * owned <= 128
    rows = -(-(3 + owned) // 8) * 8
    smem = pl.BlockSpec(memory_space=pltpu.SMEM)
    vmem = pl.BlockSpec(memory_space=pltpu.VMEM)
    whole = pl.BlockSpec(memory_space=pl.ANY)
    dma = pltpu.SemaphoreType.DMA
    out = pl.pallas_call(
        kernel,
        out_shape=jax.ShapeDtypeStruct((rows, 128), F32),
        in_specs=[whole, whole, smem, smem, smem, smem, smem, vmem, vmem, vmem],
        out_specs=vmem,
        scratch_shapes=[
            pltpu.VMEM((slab, width, width), jnp.int32),
            pltpu.VMEM((slab, width, width), F32),
            pltpu.VMEM((slab, width, width), F32),
            pltpu.VMEM((slab + 2, width, width), F32),
            pltpu.VMEM((slab + 2, width + 2 * PAD, width), F32),
            pltpu.VMEM((slabs, 2, width, width), F32),
            pltpu.VMEM((groups, 8, 128), F32),
            pltpu.VMEM((slabs, STATS, 128), F32),
            pltpu.VMEM((groups, STATS, 128), F32),
            dma((2, slab // GROUP)),
            dma((slabs,)),
            dma((slabs,)),
            dma((groups,)),
            dma((groups,)),
            dma((slabs,)),
            dma((slabs,)),
            dma((groups,)),
            dma((groups,)),
        ],
        compiler_params=pltpu.CompilerParams(
            collective_id=0, has_side_effects=True, vmem_limit_bytes=48 << 20
        ),
    )(ids, fiber, phases, theta, corners, positions, choices, right, left, modes)
    return out[:3, 0].reshape(1, 3), out[3 : 3 + owned, 0]


def solution(mesh):
    groups, slabs = mesh.shape["macro"], mesh.shape["pencil"]
    in_specs = (
        P("macro", "pencil", None, None),
        P("macro", "pencil", None, None),
        P("macro", None),
        P("macro"),
        P("macro", None),
        P("macro"),
        P("macro"),
    )
    out_specs = (P("macro", None), P("macro"))

    def run(ids, fiber, *rest):
        width = fiber.shape[3]
        right, left = hartley_tables(width)
        modes = mode_tables(width, fiber.shape[1] // slabs)
        body = functools.partial(
            on_device, jnp.asarray(right), jnp.asarray(left), jnp.asarray(modes), groups, slabs
        )
        return jax.shard_map(
            body, mesh=mesh, in_specs=in_specs, out_specs=out_specs, check_vma=False
        )(ids, fiber, *rest)

    return run
```

time: 577 us -> 45.7 us (0.08); the launches traced: 569 us -> 45.4 us
  blocking collectives: 163 us -> 0 us
  waiting for transfers between devices: 150 us -> 0 us
  matrix products: 102 us -> 0 us
  local copies, waits for them, and re-layouts: 61.3 us -> 9.8 us
  starting transfers between devices: 49.1 us -> 0 us
  Pallas kernels: 0 us -> 34.3 us
  other arithmetic: 31.9 us -> 0 us
  between operations: 11.5 us -> 1.3 us
    unnamed x5 -> x0, blocking collectives: 148 us -> none
    all_to_all x10 -> x0, waiting for transfers between devices: 145 us -> none  [the longest x2 44.9 us: forward_spectrum(): lax.all_to_all(imag_part, 'pencil', split_axis=1, concat_axis=0, tiled=True)]
    dot_general x42 -> x0, matrix products: 102 us -> none  [the longest x8 21.8 us: complex_transform_pass(): real_sin = jnp.einsum(form, real_part, sine, precision=HIGHEST)]
    all_to_all x10 -> x0, starting transfers between devices: 47.4 us -> none  [the longest x2 9.51 us: inverse_field(): lax.all_to_all(real_part, 'pencil', split_axis=0, concat_axis=1, tiled=True)]
    pallas_call x0 -> x1, Pallas kernels: none -> 34.3 us  [on_device(): pl.pallas_call(kernel, out_shape=jax.ShapeDtypeStruct((rows, 128), F32),...]
    all_to_all x8 -> x0, local copies, waits for them, and re-layouts: 17.1 us -> none  [the longest x2 6.37 us: forward_spectrum(): lax.all_to_all(real_part, 'pencil', split_axis=1, concat_axis=0, tiled=True)]
    psum x2 -> x0, blocking collectives: 14.8 us -> none  [the longest x1 7.44 us: solve_slot(): flux = lax.psum(local, 'pencil') / volume]
    reduce_sum x10 -> x0, other arithmetic: 14 us -> none  [the longest x1 6.97 us: on_device(): totals = lax.psum((jnp.sum(conduct), jnp.sum(conduct * conduct)), 'pencil')]
  transfers between devices with their start and end apart: 14 -> 0, of which waited for: 12 -> 0; matrix products, arithmetic and copies ran while one was open for 13% -> 0% of each run, Pallas kernels for 0% -> 0%
where the time goes in v1:
time: 45.7 us; the launch traced here: 45.4 us
  Pallas kernels  34.3 us (75%)
  local copies, waits for them, and re-layouts  9.8 us (21%)
  between operations  1.3 us (3%)
    pallas_call x1, Pallas kernels, on_device(): pl.pallas_call(kernel, out_shape=jax.ShapeDtypeStruct((rows, 128), F32),...  34.3 us
    unnamed x18, local copies, waits for them, and re-layouts  8.55 us
    slice x2, local copies, waits for them, and re-layouts, on_device(): return (out[:3, 0].reshape(1, 3), out[3:3 + owned, 0])  1.25 us

profile of v1, /device:TPU:0, one launch (start us, length us, event | category | flops | bytes accessed | tf_op | source)
XLA Modules:
  0.0 45.4 jit_solution(10489632199566974344)
XLA Ops:
  1.3 0.0 copy-start
  1.3 1.6 %copy-done = s32[1,32,128,128]{3,2,1,0:T(8,128)S(1)} copy-done((s32[1,32,128,128]{3,2,1,0:T(8,128)S(1)}, s32[1,32,128,128]{3,2,1,0:T(8,128)}, u32[]{:S(2)}) %copy-start) | copy-done | bytes 2097176
  2.9 0.0 copy-start.1
  2.9 1.6 %copy-done.1 = f32[1,32,128,128]{3,2,1,0:T(8,128)S(1)} copy-done((f32[1,32,128,128]{3,2,1,0:T(8,128)S(1)}, f32[1,32,128,128]{3,2,1,0:T(8,128)}, u32[]{:S(2)}) %copy-start.1) | copy-done | bytes 2097176
  4.5 0.0 copy-start.2
  4.5 0.9 %copy-done.2 = f32[4,128,128]{2,1,0:T(8,128)S(1)} copy-done((f32[4,128,128]{2,1,0:T(8,128)S(1)}, f32[4,128,128]{2,1,0:T(8,128)}, u32[]{:S(2)}) %copy-start.2) | copy-done | bytes 262168
  5.4 0.0 copy-start.3
  5.4 0.9 %copy-done.3 = bf16[256,256]{1,0:T(8,128)(2,1)S(1)} copy-done((bf16[256,256]{1,0:T(8,128)(2,1)S(1)}, bf16[256,256]{1,0:T(8,128)(2,1)}, u32[]{:S(2)}) %copy-start.3) | copy-done | bytes 131096
  6.3 0.0 copy-start.4
  6.3 0.9 %copy-done.4 = bf16[256,256]{1,0:T(8,128)(2,1)S(1)} copy-done((bf16[256,256]{1,0:T(8,128)(2,1)S(1)}, bf16[256,256]{1,0:T(8,128)(2,1)}, u32[]{:S(2)}) %copy-start.4) | copy-done | bytes 131096
  7.2 0.0 copy-start.5
  7.2 0.7 %copy-done.5 = f32[1,3]{1,0:T(1,128)S(1)} copy-done((f32[1,3]{1,0:T(1,128)S(1)}, f32[1,3]{1,0:T(1,128)}, u32[]{:S(2)}) %copy-start.5) | copy-done | bytes 36
  7.9 0.0 copy-start.6
  7.9 0.7 %copy-done.6 = f32[4]{0:T(128)S(1)} copy-done((f32[4]{0:T(128)S(1)}, f32[4]{0:T(128)}, u32[]{:S(2)}) %copy-start.6) | copy-done | bytes 40
  8.5 0.0 copy-start.7
  8.5 0.7 %copy-done.7 = s32[1,8]{1,0:T(1,128)S(1)} copy-done((s32[1,8]{1,0:T(1,128)S(1)}, s32[1,8]{1,0:T(1,128)}, u32[]{:S(2)}) %copy-start.7) | copy-done | bytes 56
  9.2 0.0 copy-start.8
  9.2 0.7 %copy-done.8 = s32[4]{0:T(128)S(1)} copy-done((s32[4]{0:T(128)S(1)}, s32[4]{0:T(128)}, u32[]{:S(2)}) %copy-start.8) | copy-done | bytes 40
  9.8 34.3 %shard_map.113 = f32[8,128]{1,0:T(8,128)S(1)} custom-call(s32[1,32,128,128]{3,2,1,0:T(8,128)S(1)} %copy-done, f32[1,32,128,128]{3,2,1,0:T(8,128)S(1)} %copy-done.1, f32[1,3]{1,0:T(1,128)S(1)} %copy-done.5, f32[4]{0:T(128)S(1)} %copy-done.6, s32[1,8]{1,0:T(1,128)S(1)} %copy-done.7, s32[4]{0:T(128)S(1)} %copy-done.8, s32[1]{0:T(128)S(6)} %copy.12.choice_ref, ...), custom_call_target="tpu_custom_call" | custom-call | tf_op jit(solution)/shard_map/pallas_call | solution.py:372
  44.1 0.6 %slice_reduce_fusion = f32[4]{0:T(128)} fusion(f32[8,128]{1,0:T(8,128)S(1)} %shard_map.113), kind=kLoop, calls=%fused_computation | loop fusion | bytes 32 | tf_op jit(solution)/shard_map/slice | solution.py:401
  44.8 0.6 %slice_reduce_fusion.1 = f32[3]{0:T(128)} fusion(f32[8,128]{1,0:T(8,128)S(1)} %shard_map.113), kind=kLoop, calls=%fused_computation.1 | loop fusion | bytes 24 | tf_op jit(solution)/shard_map/slice | solution.py:401
Async XLA Ops:
  1.3 1.6 %copy-start = (s32[1,32,128,128]{3,2,1,0:T(8,128)S(1)}, s32[1,32,128,128]{3,2,1,0:T(8,128)}, u32[]{:S(2)}) copy-start(s32[1,32,128,128]{3,2,1,0:T(8,128)} %ids_hbm.1) | copy-start | bytes 6291460
  2.9 1.6 %copy-start.1 = (f32[1,32,128,128]{3,2,1,0:T(8,128)S(1)}, f32[1,32,128,128]{3,2,1,0:T(8,128)}, u32[]{:S(2)}) copy-start(f32[1,32,128,128]{3,2,1,0:T(8,128)} %fiber_hbm.1) | copy-start | bytes 6291460
  4.5 0.9 %copy-start.2 = (f32[4,128,128]{2,1,0:T(8,128)S(1)}, f32[4,128,128]{2,1,0:T(8,128)}, u32[]{:S(2)}) copy-start(f32[4,128,128]{2,1,0:T(8,128)} %constant.8.clone.modes_ref) | copy-start | bytes 786436
  5.4 0.9 %copy-start.3 = (bf16[256,256]{1,0:T(8,128)(2,1)S(1)}, bf16[256,256]{1,0:T(8,128)(2,1)}, u32[]{:S(2)}) copy-start(bf16[256,256]{1,0:T(8,128)(2,1)} %constant.7.clone.left_ref) | copy-start | bytes 393220
  6.3 0.9 %copy-start.4 = (bf16[256,256]{1,0:T(8,128)(2,1)S(1)}, bf16[256,256]{1,0:T(8,128)(2,1)}, u32[]{:S(2)}) copy-start(bf16[256,256]{1,0:T(8,128)(2,1)} %constant.6.clone.right_ref) | copy-start | bytes 393220
  7.2 0.7 %copy-start.5 = (f32[1,3]{1,0:T(1,128)S(1)}, f32[1,3]{1,0:T(1,128)}, u32[]{:S(2)}) copy-start(f32[1,3]{1,0:T(1,128)} %phase_ref.1) | copy-start | bytes 40
  7.9 0.7 %copy-start.6 = (f32[4]{0:T(128)S(1)}, f32[4]{0:T(128)}, u32[]{:S(2)}) copy-start(f32[4]{0:T(128)} %theta_ref.1) | copy-start | bytes 52
  8.5 0.7 %copy-start.7 = (s32[1,8]{1,0:T(1,128)S(1)}, s32[1,8]{1,0:T(1,128)}, u32[]{:S(2)}) copy-start(s32[1,8]{1,0:T(1,128)} %corner_ref.1) | copy-start | bytes 100
  9.2 0.7 %copy-start.8 = (s32[4]{0:T(128)S(1)}, s32[4]{0:T(128)}, u32[]{:S(2)}) copy-start(s32[4]{0:T(128)} %position_ref.1) | copy-start | bytes 52

commit v2 on v1

--- a/solution.py
+++ b/solution.py
@@ -71,6 +71,15 @@
 def kernel(
     ids_hbm,
     fiber_hbm,
+    phase_hbm,
+    theta_hbm,
+    corner_hbm,
+    position_hbm,
+    choice_hbm,
+    right_hbm,
+    left_hbm,
+    modes_hbm,
+    out_ref,
     phase_ref,
     theta_ref,
     corner_ref,
@@ -79,7 +88,6 @@
     right_ref,
     left_ref,
     modes_ref,
-    out_ref,
     ids_ref,
     conduct_ref,
     spectrum_ref,
@@ -89,6 +97,7 @@
     info_ref,
     part_ref,
     stat_ref,
+    small_sem,
     load_sem,
     moment_send,
     moment_recv,
@@ -114,7 +123,24 @@
             ),
         )
 
-    for step in range(slab // GROUP):
+    small = [
+        pltpu.make_async_copy(source, target, small_sem.at[i])
+        for i, (source, target) in enumerate(
+            (
+                (phase_hbm, phase_ref),
+                (right_hbm, right_ref),
+                (left_hbm, left_ref),
+                (modes_hbm, modes_ref),
+                (theta_hbm, theta_ref),
+                (corner_hbm, corner_ref),
+                (position_hbm, position_ref),
+                (choice_hbm, choice_ref),
+            )
+        )
+    ]
+    for copy in small[:3] + list(loads(0)) + small[3:]:
+        copy.start()
+    for step in range(1, slab // GROUP):
         for load in loads(step):
             load.start()
 
@@ -141,6 +167,8 @@
             for k in range(1, size)
         ]
 
+    for copy in small:
+        copy.wait()
     lane = lax.broadcasted_iota(jnp.int32, (1, 128), 1)
     hits = [jnp.where(lane == corner_ref[0, a], 1.0, 0.0) for a in range(8)]
     info = []
@@ -365,16 +393,23 @@
     owned = theta.shape[0]
     assert corners.shape[0] == 1 and groups * owned <= 128
     rows = -(-(3 + owned) // 8) * 8
-    smem = pl.BlockSpec(memory_space=pltpu.SMEM)
     vmem = pl.BlockSpec(memory_space=pltpu.VMEM)
-    whole = pl.BlockSpec(memory_space=pl.ANY)
+    whole = pl.BlockSpec(memory_space=pltpu.HBM)
     dma = pltpu.SemaphoreType.DMA
     out = pl.pallas_call(
         kernel,
         out_shape=jax.ShapeDtypeStruct((rows, 128), F32),
-        in_specs=[whole, whole, smem, smem, smem, smem, smem, vmem, vmem, vmem],
+        in_specs=[whole] * 10,
         out_specs=vmem,
         scratch_shapes=[
+            pltpu.SMEM(phases.shape, F32),
+            pltpu.SMEM(theta.shape, F32),
+            pltpu.SMEM(corners.shape, jnp.int32),
+            pltpu.SMEM(positions.shape, jnp.int32),
+            pltpu.SMEM(choices.shape, jnp.int32),
+            pltpu.VMEM(right.shape, BF16),
+            pltpu.VMEM(left.shape, BF16),
+            pltpu.VMEM(modes.shape, F32),
             pltpu.VMEM((slab, width, width), jnp.int32),
             pltpu.VMEM((slab, width, width), F32),
             pltpu.VMEM((slab, width, width), F32),
@@ -384,6 +419,7 @@
             pltpu.VMEM((groups, 8, 128), F32),
             pltpu.VMEM((slabs, STATS, 128), F32),
             pltpu.VMEM((groups, STATS, 128), F32),
+            dma((8,)),
             dma((2, slab // GROUP)),
             dma((slabs,)),
             dma((slabs,)),
@@ -395,7 +431,7 @@
             dma((groups,)),
         ],
         compiler_params=pltpu.CompilerParams(
-            collective_id=0, has_side_effects=True, vmem_limit_bytes=48 << 20
+            collective_id=0, has_side_effects=True, vmem_limit_bytes=60 << 20
         ),
     )(ids, fiber, phases, theta, corners, positions, choices, right, left, modes)
     return out[:3, 0].reshape(1, 3), out[3 : 3 + owned, 0]

time: 45.7 us -> 40.1 us (0.88)
  local copies, waits for them, and re-layouts: 9.8 us -> 2.62 us
  Pallas kernels: 34.3 us -> 36 us
    unnamed x18 -> x0, local copies, waits for them, and re-layouts: 8.55 us -> none
    pallas_call x1, Pallas kernels: 34.3 us -> 36 us  [on_device(): pl.pallas_call(kernel, out_shape=jax.ShapeDtypeStruct((rows, 128), F32),...]
    slice x2, local copies, waits for them, and re-layouts: 1.25 us -> 2.62 us  [on_device(): return (out[:3, 0].reshape(1, 3), out[3:3 + owned, 0])]
where the time goes in v2:
time: 40.1 us; the launch traced here: 39.9 us
  Pallas kernels  36 us (90%)
  local copies, waits for them, and re-layouts  2.62 us (7%)
  between operations  1.29 us (3%)
    pallas_call x1, Pallas kernels, on_device(): pl.pallas_call(kernel, out_shape=jax.ShapeDtypeStruct((rows, 128), F32),...  36 us
    slice x2, local copies, waits for them, and re-layouts, on_device(): return (out[:3, 0].reshape(1, 3), out[3:3 + owned, 0])  2.62 us

profile of v2, /device:TPU:0, one launch (start us, length us, event | category | flops | bytes accessed | tf_op | source)
XLA Modules:
  0.0 39.9 jit_solution(18226845089172012209)
XLA Ops:
  1.3 36.0 %shard_map.113 = f32[8,128]{1,0:T(8,128)} custom-call(s32[1,32,128,128]{3,2,1,0:T(8,128)} %ids_hbm.1, f32[1,32,128,128]{3,2,1,0:T(8,128)} %fiber_hbm.1, f32[1,3]{1,0:T(1,128)} %phase_hbm.1, f32[4]{0:T(128)} %theta_hbm.1, s32[1,8]{1,0:T(1,128)} %corner_hbm.1, s32[4]{0:T(128)} %position_hbm.1, s32[1]{0:T(128)S(6)} %copy.12.choice_hbm, ...), custom_call_target="tpu_custom_call" | custom-call | tf_op jit(solution)/shard_map/pallas_call | solution.py:399
  37.3 1.3 %slice_reduce_fusion = f32[4]{0:T(128)} fusion(f32[8,128]{1,0:T(8,128)} %shard_map.113), kind=kLoop, calls=%fused_computation | loop fusion | bytes 32 | tf_op jit(solution)/shard_map/slice | solution.py:437
  38.6 1.3 %slice_reduce_fusion.1 = f32[3]{0:T(128)} fusion(f32[8,128]{1,0:T(8,128)} %shard_map.113), kind=kLoop, calls=%fused_computation.1 | loop fusion | bytes 24 | tf_op jit(solution)/shard_map/slice | solution.py:437

commit v3 on v2

--- a/solution.py
+++ b/solution.py
@@ -17,6 +17,7 @@
 STATS = 16
 PAD = 8
 BLOCK = 32
+ROWS = 8
 
 
 def hartley_tables(width):
@@ -59,6 +60,22 @@
         second = both[(2 * pair + 1) * width : (2 * pair + 2) * width]
         high, low = split(jnp.concatenate([first, second], axis=1))
         result = jnp.dot(left, jnp.concatenate([high, low], axis=0), preferred_element_type=F32)
+        result = result[:width] + result[width:]
+        planes += [result[:, :width], result[:, width:]]
+    return planes
+
+
+def forward_plane_pass(x, right, left):
+    count, width = x.shape[0], x.shape[2]
+    flat = x.reshape(count * width, width).astype(BF16)
+    both = jnp.dot(flat, right[:width], preferred_element_type=F32)
+    both = (both[:, :width] + both[:, width:]).astype(BF16)
+    planes = []
+    for pair in range(count // 2):
+        first = both[2 * pair * width : (2 * pair + 1) * width]
+        second = both[(2 * pair + 1) * width : (2 * pair + 2) * width]
+        data = jnp.concatenate([first, second], axis=1)
+        result = jnp.dot(left[:, :width], data, preferred_element_type=F32)
         result = result[:width] + result[width:]
         planes += [result[:, :width], result[:, width:]]
     return planes
@@ -200,7 +217,7 @@
         total = total + fold(flat)
         square = square + fold(flat * flat)
         scale = modes_ref[1]
-        for i, plane in enumerate(hartley_plane_pass(value, right_ref[...], left_ref[...])):
+        for i, plane in enumerate(forward_plane_pass(value, right_ref[...], left_ref[...])):
             spectrum_ref[step * GROUP + i] = plane * scale
         return total, square
 
@@ -223,6 +240,10 @@
         return carry
 
     lax.fori_loop(0, width // BLOCK, moments, 0)
+    first = (lax.broadcasted_iota(jnp.int32, (8, width), 0) == 0) & (
+        lax.broadcasted_iota(jnp.int32, (8, width), 1) == 0
+    )
+    moment_ref[0, 0, :8] = jnp.where(first, jnp.sum(total) * (1.0 / volume), moment_ref[0, 0, :8])
 
     pl.semaphore_wait(barrier, groups + slabs - 2)
     moment_copies = ring(
@@ -237,9 +258,6 @@
         copy.wait()
 
     corner = sum(moment_ref[k, 0, :8, :] for k in range(slabs))
-    first = (lax.broadcasted_iota(jnp.int32, (8, width), 0) == 0) & (
-        lax.broadcasted_iota(jnp.int32, (8, width), 1) == 0
-    )
     mean = jnp.sum(jnp.where(first, corner, 0.0))
 
     def solve(block, carry):
@@ -295,15 +313,15 @@
 
     def contract(x, sums):
         sums = list(sums)
-        for block in range(width // BLOCK):
+        for block in range(width // ROWS):
 
             def at(plane, shift):
-                return field_ref[plane, PAD + block * BLOCK + shift : PAD + (block + 1) * BLOCK + shift, :]
+                return field_ref[plane, PAD + block * ROWS + shift : PAD + (block + 1) * ROWS + shift, :]
 
             here, south, north = at(x + 1, 0), at(x + 1, -1), at(x + 1, 1)
             east, east_south = at(x + 2, 0), at(x + 2, -1)
             west, west_north = at(x, 0), at(x, 1)
-            value = conduct_ref[x, block * BLOCK : (block + 1) * BLOCK, :]
+            value = conduct_ref[x, block * ROWS : (block + 1) * ROWS, :]
             in_y, next_y = here - south, north - here
             out_x, into_x = east - here, here - west
             yy = next_y - in_y
@@ -431,7 +449,7 @@
             dma((groups,)),
         ],
         compiler_params=pltpu.CompilerParams(
-            collective_id=0, has_side_effects=True, vmem_limit_bytes=60 << 20
+            collective_id=0, has_side_effects=True, vmem_limit_bytes=20 << 20
         ),
     )(ids, fiber, phases, theta, corners, positions, choices, right, left, modes)
     return out[:3, 0].reshape(1, 3), out[3 : 3 + owned, 0]

time: 40.1 us -> 45.4 us (1.13)
  local copies, waits for them, and re-layouts: 2.62 us -> 9.8 us
  Pallas kernels: 36 us -> 34 us
    unnamed x0 -> x18, local copies, waits for them, and re-layouts: none -> 8.55 us
    pallas_call x1, Pallas kernels: 36 us -> 34 us  [on_device(): pl.pallas_call(kernel, out_shape=jax.ShapeDtypeStruct((rows, 128), F32),...]
    slice x2, local copies, waits for them, and re-layouts: 2.62 us -> 1.25 us  [on_device(): return (out[:3, 0].reshape(1, 3), out[3:3 + owned, 0])]
where the time goes in v3:
time: 45.4 us; the launch traced here: 45.1 us
  Pallas kernels  34 us (75%)
  local copies, waits for them, and re-layouts  9.8 us (22%)
  between operations  1.3 us (3%)
    pallas_call x1, Pallas kernels, on_device(): pl.pallas_call(kernel, out_shape=jax.ShapeDtypeStruct((rows, 128), F32),...  34 us
    unnamed x18, local copies, waits for them, and re-layouts  8.55 us
    slice x2, local copies, waits for them, and re-layouts, on_device(): return (out[:3, 0].reshape(1, 3), out[3:3 + owned, 0])  1.25 us

profile of v3, /device:TPU:0, one launch (start us, length us, event | category | flops | bytes accessed | tf_op | source)
XLA Modules:
  0.0 45.1 jit_solution(2494626170599290223)
XLA Ops:
  1.3 0.0 copy-start
  1.3 1.6 %copy-done = s32[1,32,128,128]{3,2,1,0:T(8,128)S(1)} copy-done((s32[1,32,128,128]{3,2,1,0:T(8,128)S(1)}, s32[1,32,128,128]{3,2,1,0:T(8,128)}, u32[]{:S(2)}) %copy-start) | copy-done | bytes 2097176
  2.9 0.0 copy-start.1
  2.9 1.6 %copy-done.1 = f32[1,32,128,128]{3,2,1,0:T(8,128)S(1)} copy-done((f32[1,32,128,128]{3,2,1,0:T(8,128)S(1)}, f32[1,32,128,128]{3,2,1,0:T(8,128)}, u32[]{:S(2)}) %copy-start.1) | copy-done | bytes 2097176
  4.5 0.0 copy-start.2
  4.5 0.9 %copy-done.2 = f32[4,128,128]{2,1,0:T(8,128)S(1)} copy-done((f32[4,128,128]{2,1,0:T(8,128)S(1)}, f32[4,128,128]{2,1,0:T(8,128)}, u32[]{:S(2)}) %copy-start.2) | copy-done | bytes 262168
  5.4 0.0 copy-start.3
  5.4 0.9 %copy-done.3 = bf16[256,256]{1,0:T(8,128)(2,1)S(1)} copy-done((bf16[256,256]{1,0:T(8,128)(2,1)S(1)}, bf16[256,256]{1,0:T(8,128)(2,1)}, u32[]{:S(2)}) %copy-start.3) | copy-done | bytes 131096
  6.3 0.0 copy-start.4
  6.3 0.9 %copy-done.4 = bf16[256,256]{1,0:T(8,128)(2,1)S(1)} copy-done((bf16[256,256]{1,0:T(8,128)(2,1)S(1)}, bf16[256,256]{1,0:T(8,128)(2,1)}, u32[]{:S(2)}) %copy-start.4) | copy-done | bytes 131096
  7.2 0.0 copy-start.5
  7.2 0.7 %copy-done.5 = f32[1,3]{1,0:T(1,128)S(1)} copy-done((f32[1,3]{1,0:T(1,128)S(1)}, f32[1,3]{1,0:T(1,128)}, u32[]{:S(2)}) %copy-start.5) | copy-done | bytes 36
  7.9 0.0 copy-start.6
  7.9 0.7 %copy-done.6 = f32[4]{0:T(128)S(1)} copy-done((f32[4]{0:T(128)S(1)}, f32[4]{0:T(128)}, u32[]{:S(2)}) %copy-start.6) | copy-done | bytes 40
  8.5 0.0 copy-start.7
  8.5 0.7 %copy-done.7 = s32[1,8]{1,0:T(1,128)S(1)} copy-done((s32[1,8]{1,0:T(1,128)S(1)}, s32[1,8]{1,0:T(1,128)}, u32[]{:S(2)}) %copy-start.7) | copy-done | bytes 56
  9.2 0.0 copy-start.8
  9.2 0.7 %copy-done.8 = s32[4]{0:T(128)S(1)} copy-done((s32[4]{0:T(128)S(1)}, s32[4]{0:T(128)}, u32[]{:S(2)}) %copy-start.8) | copy-done | bytes 40
  9.8 34.0 %shard_map.113 = f32[8,128]{1,0:T(8,128)S(1)} custom-call(s32[1,32,128,128]{3,2,1,0:T(8,128)S(1)} %copy-done, f32[1,32,128,128]{3,2,1,0:T(8,128)S(1)} %copy-done.1, f32[1,3]{1,0:T(1,128)S(1)} %copy-done.5, f32[4]{0:T(128)S(1)} %copy-done.6, s32[1,8]{1,0:T(1,128)S(1)} %copy-done.7, s32[4]{0:T(128)S(1)} %copy-done.8, s32[1]{0:T(128)S(6)} %copy.12.choice_hbm, ...), custom_call_target="tpu_custom_call" | custom-call | tf_op jit(solution)/shard_map/pallas_call | solution.py:417
  43.8 0.6 %slice_reduce_fusion = f32[4]{0:T(128)} fusion(f32[8,128]{1,0:T(8,128)S(1)} %shard_map.113), kind=kLoop, calls=%fused_computation | loop fusion | bytes 32 | tf_op jit(solution)/shard_map/slice | solution.py:455
  44.4 0.6 %slice_reduce_fusion.1 = f32[3]{0:T(128)} fusion(f32[8,128]{1,0:T(8,128)S(1)} %shard_map.113), kind=kLoop, calls=%fused_computation.1 | loop fusion | bytes 24 | tf_op jit(solution)/shard_map/slice | solution.py:455
Async XLA Ops:
  1.3 1.6 %copy-start = (s32[1,32,128,128]{3,2,1,0:T(8,128)S(1)}, s32[1,32,128,128]{3,2,1,0:T(8,128)}, u32[]{:S(2)}) copy-start(s32[1,32,128,128]{3,2,1,0:T(8,128)} %ids_hbm.1) | copy-start | bytes 6291460
  2.9 1.6 %copy-start.1 = (f32[1,32,128,128]{3,2,1,0:T(8,128)S(1)}, f32[1,32,128,128]{3,2,1,0:T(8,128)}, u32[]{:S(2)}) copy-start(f32[1,32,128,128]{3,2,1,0:T(8,128)} %fiber_hbm.1) | copy-start | bytes 6291460
  4.5 0.9 %copy-start.2 = (f32[4,128,128]{2,1,0:T(8,128)S(1)}, f32[4,128,128]{2,1,0:T(8,128)}, u32[]{:S(2)}) copy-start(f32[4,128,128]{2,1,0:T(8,128)} %constant.8.clone.modes_hbm) | copy-start | bytes 786436
  5.4 0.9 %copy-start.3 = (bf16[256,256]{1,0:T(8,128)(2,1)S(1)}, bf16[256,256]{1,0:T(8,128)(2,1)}, u32[]{:S(2)}) copy-start(bf16[256,256]{1,0:T(8,128)(2,1)} %constant.7.clone.left_hbm) | copy-start | bytes 393220
  6.3 0.9 %copy-start.4 = (bf16[256,256]{1,0:T(8,128)(2,1)S(1)}, bf16[256,256]{1,0:T(8,128)(2,1)}, u32[]{:S(2)}) copy-start(bf16[256,256]{1,0:T(8,128)(2,1)} %constant.6.clone.right_hbm) | copy-start | bytes 393220
  7.2 0.7 %copy-start.5 = (f32[1,3]{1,0:T(1,128)S(1)}, f32[1,3]{1,0:T(1,128)}, u32[]{:S(2)}) copy-start(f32[1,3]{1,0:T(1,128)} %phase_hbm.1) | copy-start | bytes 40
  7.9 0.7 %copy-start.6 = (f32[4]{0:T(128)S(1)}, f32[4]{0:T(128)}, u32[]{:S(2)}) copy-start(f32[4]{0:T(128)} %theta_hbm.1) | copy-start | bytes 52
  8.5 0.7 %copy-start.7 = (s32[1,8]{1,0:T(1,128)S(1)}, s32[1,8]{1,0:T(1,128)}, u32[]{:S(2)}) copy-start(s32[1,8]{1,0:T(1,128)} %corner_hbm.1) | copy-start | bytes 100
  9.2 0.7 %copy-start.8 = (s32[4]{0:T(128)S(1)}, s32[4]{0:T(128)}, u32[]{:S(2)}) copy-start(s32[4]{0:T(128)} %position_hbm.1) | copy-start | bytes 52

commit v4 on v3

--- a/solution.py
+++ b/solution.py
@@ -449,7 +449,7 @@
             dma((groups,)),
         ],
         compiler_params=pltpu.CompilerParams(
-            collective_id=0, has_side_effects=True, vmem_limit_bytes=20 << 20
+            collective_id=0, has_side_effects=True, vmem_limit_bytes=60 << 20
         ),
     )(ids, fiber, phases, theta, corners, positions, choices, right, left, modes)
     return out[:3, 0].reshape(1, 3), out[3 : 3 + owned, 0]

time: 45.4 us -> 39.7 us (0.87)
  local copies, waits for them, and re-layouts: 9.8 us -> 2.62 us
  Pallas kernels: 34 us -> 35.6 us
    unnamed x18 -> x0, local copies, waits for them, and re-layouts: 8.55 us -> none
    pallas_call x1, Pallas kernels: 34 us -> 35.6 us  [on_device(): pl.pallas_call(kernel, out_shape=jax.ShapeDtypeStruct((rows, 128), F32),...]
    slice x2, local copies, waits for them, and re-layouts: 1.25 us -> 2.62 us  [on_device(): return (out[:3, 0].reshape(1, 3), out[3:3 + owned, 0])]
where the time goes in v4:
time: 39.7 us; the launch traced here: 39.5 us
  Pallas kernels  35.6 us (90%)
  local copies, waits for them, and re-layouts  2.62 us (7%)
  between operations  1.29 us (3%)
    pallas_call x1, Pallas kernels, on_device(): pl.pallas_call(kernel, out_shape=jax.ShapeDtypeStruct((rows, 128), F32),...  35.6 us
    slice x2, local copies, waits for them, and re-layouts, on_device(): return (out[:3, 0].reshape(1, 3), out[3:3 + owned, 0])  2.62 us

profile of v4, /device:TPU:0, one launch (start us, length us, event | category | flops | bytes accessed | tf_op | source)
XLA Modules:
  0.0 39.5 jit_solution(14427514408015344362)
XLA Ops:
  1.3 35.6 %shard_map.113 = f32[8,128]{1,0:T(8,128)} custom-call(s32[1,32,128,128]{3,2,1,0:T(8,128)} %ids_hbm.1, f32[1,32,128,128]{3,2,1,0:T(8,128)} %fiber_hbm.1, f32[1,3]{1,0:T(1,128)} %phase_hbm.1, f32[4]{0:T(128)} %theta_hbm.1, s32[1,8]{1,0:T(1,128)} %corner_hbm.1, s32[4]{0:T(128)} %position_hbm.1, s32[1]{0:T(128)S(6)} %copy.12.choice_hbm, ...), custom_call_target="tpu_custom_call" | custom-call | tf_op jit(solution)/shard_map/pallas_call | solution.py:417
  36.9 1.3 %slice_reduce_fusion = f32[4]{0:T(128)} fusion(f32[8,128]{1,0:T(8,128)} %shard_map.113), kind=kLoop, calls=%fused_computation | loop fusion | bytes 32 | tf_op jit(solution)/shard_map/slice | solution.py:455
  38.2 1.3 %slice_reduce_fusion.1 = f32[3]{0:T(128)} fusion(f32[8,128]{1,0:T(8,128)} %shard_map.113), kind=kLoop, calls=%fused_computation.1 | loop fusion | bytes 24 | tf_op jit(solution)/shard_map/slice | solution.py:455
